TPU v7x, 32 devices: a whole 2x2x4 slice. The times are simulated.
32 devices in a mesh: dp: 8 (over z, y), head: 4 (over x, core).
Axes of the slice: x: 2, y: 2, z: 4, core: 2. Of those that a mesh axis runs over, the one named last changes fastest.
Arguments:
- inputs: bfloat16 [8192, 2048], P('dp', 'head'), may hold values from -6 to 6
- cotangent: bfloat16 [8192, 2048], P('dp', 'head'), may hold values from -6 to 6
- token_valid: int32 [8192], P('dp'), may hold values from 0 to 1, as said below
- block_opens: int32 [32], P('dp'), may hold values from 0 to 1, as said below
- block_widths: int32 [32], P('dp'), may hold values from 16 to 64, as said below
- weight_inner: float32 [2048, 2, 4096], P('dp', None, 'head'), may hold values from -0.125 to 0.125
- weight_step: float32 [2048, 64], P('dp', 'head'), may hold values from -0.125 to 0.125
- weight_output: float32 [4096, 2048], P('head', 'dp'), may hold values from -0.09375 to 0.09375
- weight_state: float32 [2048, 256], P(('dp', 'head')), may hold values from -0.125 to 0.125
- norm_gain: float32 [2048], P(('dp', 'head')), may hold values from 0.5 to 1.5
- channel_table: float32 [6, 4096], P(None, 'head'), may hold values from -1.5 to 1.5, as said below
- head_table: float32 [3, 64], P(None, 'head'), may hold values from -9 to 1.5
- state_filter: float32 [256, 5], P(('dp', 'head')), may hold values from -2.5 to 2.5
- momentum_inner: float32 [2048, 2, 4096], P('dp', None, 'head'), may hold values from -112 to 112
- momentum_step: float32 [2048, 64], P('dp', 'head'), may hold values from -160 to 160
- momentum_output: float32 [4096, 2048], P('head', 'dp'), may hold values from -256 to 256
- momentum_state: float32 [2048, 256], P(('dp', 'head')), may hold values from -56 to 56
- momentum_gain: float32 [2048], P(('dp', 'head')), may hold values from -512 to 512
- momentum_channel: float32 [6, 4096], P(None, 'head'), may hold values from -256 to 256
- momentum_head: float32 [3, 64], P(None, 'head'), may hold values from -1024 to 1024
- momentum_filter: float32 [256, 5], P(('dp', 'head')), may hold values from -256 to 256
- average_inner: float32 [2048, 2, 4096], P('dp', None, 'head'), may hold values from -0.125 to 0.125
- average_step: float32 [2048, 64], P('dp', 'head'), may hold values from -0.125 to 0.125
- average_output: float32 [4096, 2048], P('head', 'dp'), may hold values from -0.09375 to 0.09375
- average_state: float32 [2048, 256], P(('dp', 'head')), may hold values from -0.125 to 0.125
- average_gain: float32 [2048], P(('dp', 'head')), may hold values from 0.5 to 1.5
- average_channel: float32 [6, 4096], P(None, 'head'), may hold values from -3 to 3
- average_head: float32 [3, 64], P(None, 'head'), may hold values from -6 to 6
- average_filter: float32 [256, 5], P(('dp', 'head')), may hold values from -3 to 3
Outputs:
- layer_output: bfloat16 [8192, 2048], P('dp', 'head')
- grad_input: float32 [8192, 2048], P('dp', 'head')
- updated_inner: float32 [2048, 2, 4096], P('dp', None, 'head')
- carried_inner: float32 [2048, 2, 4096], P('dp', None, 'head')
- smoothed_inner: float32 [2048, 2, 4096], P('dp', None, 'head')
- updated_step: float32 [2048, 64], P('dp', 'head')
- carried_step: float32 [2048, 64], P('dp', 'head')
- smoothed_step: float32 [2048, 64], P('dp', 'head')
- updated_output: float32 [4096, 2048], P('head', 'dp')
- carried_output: float32 [4096, 2048], P('head', 'dp')
- smoothed_output: float32 [4096, 2048], P('head', 'dp')
- updated_state: float32 [2048, 256], P(('dp', 'head'))
- carried_state: float32 [2048, 256], P(('dp', 'head'))
- smoothed_state: float32 [2048, 256], P(('dp', 'head'))
- updated_gain: float32 [2048], P(('dp', 'head'))
- carried_gain: float32 [2048], P(('dp', 'head'))
- smoothed_gain: float32 [2048], P(('dp', 'head'))
- updated_channel: float32 [6, 4096], P(None, 'head')
- carried_channel: float32 [6, 4096], P(None, 'head')
- smoothed_channel: float32 [6, 4096], P(None, 'head')
- updated_head: float32 [3, 64], P(None, 'head')
- carried_head: float32 [3, 64], P(None, 'head')
- smoothed_head: float32 [3, 64], P(None, 'head')
- updated_filter: float32 [256, 5], P(('dp', 'head'))
- carried_filter: float32 [256, 5], P(('dp', 'head'))
- smoothed_filter: float32 [256, 5], P(('dp', 'head'))
Inputs may be any that keep to these rules, and one draw needn't show every extreme that they name: `block_opens`: the first block of each index of dp's 1024 tokens begins a sequence; some index of dp holds one sequence of all its 1024 tokens. `block_widths`: the same for all blocks of a sequence, a multiple of 16. `token_valid`: 1 on a prefix of each sequence that covers all its blocks but the last, and 128 or more tokens of the last; 0 on the rest of that block. `channel_table`: rows 0 to 3 taps, row 4 biases, row 5 gains.
All inputs are finite; a program needn't handle non-finite values.
Results may differ from a plain program's by a relative error of at most 0.0095.
The roundings to bfloat16 on the way count: a program that leaves them out, or rounds other values in their place, can miss the bound.
Values may be sent and summed in bfloat16 or wider, within the bound.
No kernel may reach another device: no remote copies, remote signals or barrier semaphores. Data moves between devices by JAX's collectives and lax.ppermute only.
A program may use at most 192 MiB of HBM per device.

v0:
```python
import math
import jax
import jax.numpy as jnp
from jax import lax
from jax.sharding import PartitionSpec as P

D = 2048
H = 64
P_SIZE = 64
NS = 128
KC = 4
BLK = 256
EPS = 1e-05
MOMENTUM = 0.9
DECAY = 0.0001
AVERAGE = 0.75
RATE_MATRIX = 0.02
RATE_VECTOR = 0.1
HIGHEST = lax.Precision.HIGHEST


def rounded(value):
    return lax.optimization_barrier(value.astype(jnp.bfloat16)).astype(jnp.float32)


def convolve(inner_x, state_bc, taps_x, taps_bc, openings):
    joined = jnp.concatenate([inner_x, state_bc], axis=1)
    filters = jnp.concatenate([taps_x, taps_bc], axis=1)
    within = jnp.arange(joined.shape[0]) % BLK
    conv_total = filters[KC][None, :] + filters[KC - 1][None, :] * joined
    for offset in range(1, KC):
        shifted = jnp.concatenate(
            [jnp.zeros((offset, joined.shape[1]), jnp.float32), joined[:-offset]], axis=0
        )
        allowed = 1.0 - openings * (within < offset).astype(jnp.float32)
        conv_total = conv_total + filters[KC - 1 - offset][None, :] * shifted * allowed[:, None]
    active = jax.nn.silu(conv_total)
    split_at = inner_x.shape[1]
    return (active[:, :split_at], active[:, split_at:])


def state_mixer(signal_x, signal_bc, step_raw, gate_values, table, head_used, block_open):
    token_count, channels = signal_x.shape
    heads_here = table.shape[1]
    blocks_here = token_count // BLK
    step_rates = jax.nn.softplus(step_raw + table[0][None, :])
    log_rates = step_rates * (-jnp.exp(table[1]))[None, :]
    cumulated = jnp.cumsum(log_rates.reshape(blocks_here, BLK, heads_here), axis=1)
    rates_block = step_rates.reshape(blocks_here, BLK, heads_here)
    values = signal_x.reshape(blocks_here, BLK, heads_here, P_SIZE)
    inputs_map = signal_bc[:, :NS].reshape(blocks_here, BLK, NS)
    outputs_map = signal_bc[:, NS:].reshape(blocks_here, BLK, NS)
    lower_mask = (jnp.arange(BLK)[:, None] >= jnp.arange(BLK)[None, :])[None, :, :, None]
    spread = cumulated[:, :, None, :] - cumulated[:, None, :, :]
    decays = jnp.where(lower_mask, jnp.exp(jnp.where(lower_mask, spread, 0.0)), 0.0)
    intersection = jnp.einsum("nts,nus->ntu", outputs_map, inputs_map, precision=HIGHEST)
    mixing = intersection[..., None] * decays * rates_block[:, None, :, :]
    inner_part = jnp.einsum("ntuh,nuhp->nthp", mixing, values, precision=HIGHEST)
    ending = jnp.exp(cumulated[:, -1:, :] - cumulated) * rates_block
    pieces = jnp.einsum("nuh,nuhp,nus->nhps", ending, values, inputs_map, precision=HIGHEST)
    totals = jnp.exp(cumulated[:, -1, :])

    def carry_state(state_now, entries):
        piece_state, total_decay, opening = entries
        entering = state_now * (1.0 - opening)
        return (total_decay[:, None, None] * entering + piece_state, entering)

    initial = jnp.zeros((heads_here, P_SIZE, NS), jnp.float32)
    finals, entered = lax.scan(carry_state, initial, (pieces, totals, block_open))
    outer_part = jnp.exp(cumulated)[..., None] * jnp.einsum(
        "nhps,nts->nthp", entered, outputs_map, precision=HIGHEST
    )
    mixed = (inner_part + outer_part + table[2][None, None, :, None] * values) * head_used.reshape(
        blocks_here, BLK, heads_here
    )[..., None]
    gated = mixed.reshape(token_count, channels) * jax.nn.silu(gate_values)
    return (gated, jnp.sum(gated * gated, axis=1))


def gated_norm(gated, total_sq, gate_gain, norm_counts):
    norm_scale = lax.rsqrt(total_sq / norm_counts + EPS)
    return gated * norm_scale[:, None] * gate_gain[None, :]


def advance(weight, gradient, moment, average, rate):
    adjusted = gradient + DECAY * weight
    moment_next = MOMENTUM * moment + adjusted
    weight_next = weight - rate * (adjusted + MOMENTUM * moment_next)
    average_next = AVERAGE * average + (1.0 - AVERAGE) * weight_next
    return (weight_next, moment_next, average_next)


def body(
    inputs,
    cotangent,
    token_valid,
    block_opens,
    block_widths,
    weight_inner,
    weight_step,
    weight_output,
    weight_state,
    norm_gain,
    channel_table,
    head_table,
    state_filter,
    momentum_inner,
    momentum_step,
    momentum_output,
    momentum_state,
    momentum_gain,
    momentum_channel,
    momentum_head,
    momentum_filter,
    average_inner,
    average_step,
    average_output,
    average_state,
    average_gain,
    average_channel,
    average_head,
    average_filter,
):
    inner_full, step_full, output_full = (
        lax.all_gather(weight_inner.astype(jnp.bfloat16), "dp", axis=0, tiled=True),
        lax.all_gather(weight_step.astype(jnp.bfloat16), "dp", axis=0, tiled=True),
        lax.all_gather(weight_output.astype(jnp.bfloat16), "dp", axis=1, tiled=True),
    )
    state_full, gain_full, filter_full = (
        lax.all_gather(weight_state.astype(jnp.bfloat16), ("dp", "head"), axis=0, tiled=True),
        lax.all_gather(norm_gain.astype(jnp.bfloat16), ("dp", "head"), axis=0, tiled=True),
        lax.all_gather(state_filter.astype(jnp.bfloat16), ("dp", "head"), axis=0, tiled=True),
    )
    channel_used = rounded(channel_table)
    head_values = rounded(head_table)
    gathered = lax.all_gather(inputs, "head", axis=1, tiled=True)
    tokens_full = gathered.astype(jnp.float32)
    inverse = lax.rsqrt(jnp.mean(tokens_full * tokens_full, axis=1) + EPS)
    gain_float = gain_full.astype(jnp.float32)
    normed = (tokens_full * inverse[:, None] * gain_float[None, :]).astype(jnp.bfloat16)
    inner_pair = jnp.einsum("td,dkc->tkc", normed, inner_full, preferred_element_type=jnp.float32)
    gate_values = inner_pair[:, 0]
    inner_x = inner_pair[:, 1]
    state_bc = jnp.dot(normed, state_full, preferred_element_type=jnp.float32)
    step_raw = jnp.dot(normed, step_full, preferred_element_type=jnp.float32)
    block_open = block_opens.astype(jnp.float32)
    openings = jnp.repeat(block_open, BLK)
    widths = jnp.repeat(block_widths, BLK)
    heads_local = step_full.shape[1]
    head_used = (jnp.arange(heads_local)[None, :] * H < widths[:, None] * heads_local).astype(
        jnp.float32
    )
    norm_counts = widths.astype(jnp.float32) * P_SIZE
    valid_rows = token_valid.astype(jnp.float32)
    taps_x = channel_used[: KC + 1]
    gate_gain = channel_used[KC + 1]
    taps_bc = filter_full.astype(jnp.float32).T

    def conv_part(inner_value, state_value, taps_first, taps_second):
        return convolve(inner_value, state_value, taps_first, taps_second, openings)

    (conv_x, conv_bc), conv_back = jax.vjp(conv_part, inner_x, state_bc, taps_x, taps_bc)
    signal_x = rounded(conv_x)
    signal_bc = rounded(conv_bc)

    def mix_part(signal_first, signal_second, raw_steps, gate_part, table):
        return state_mixer(
            signal_first, signal_second, raw_steps, gate_part, table, head_used, block_open
        )

    (gated, local_sq), mix_back = jax.vjp(
        mix_part, signal_x, signal_bc, step_raw, gate_values, head_values
    )
    total_sq = lax.psum(local_sq, "head")

    def norm_part(gated_value, sum_value, gain_value):
        return gated_norm(gated_value, sum_value, gain_value, norm_counts)

    normalized, norm_back_fn = jax.vjp(norm_part, gated, total_sq, gate_gain)
    projected = normalized.astype(jnp.bfloat16)
    partial_out = jnp.dot(projected, output_full, preferred_element_type=jnp.float32)
    branch = lax.psum_scatter(
        partial_out.astype(jnp.bfloat16), "head", scatter_dimension=1, tiled=True
    ).astype(jnp.float32)
    own_inputs = inputs.astype(jnp.float32)
    layer_output = (own_inputs + valid_rows[:, None] * branch).astype(jnp.bfloat16)
    masked = cotangent * token_valid.astype(jnp.bfloat16)[:, None]
    shard_piece = lax.all_gather(masked, "head", axis=1, tiled=True)
    grad_normal = jnp.einsum(
        "tw,cw->tc", shard_piece, output_full, preferred_element_type=jnp.float32
    )
    block_grad = jnp.einsum("tc,tw->cw", projected, shard_piece, preferred_element_type=jnp.float32)
    grad_gated, grad_sq_part, grad_gate_gain = norm_back_fn(grad_normal)
    grad_sq = lax.psum(grad_sq_part, "head")
    grad_sx, grad_sbc, grad_raw, grad_gate, grad_head = mix_back((grad_gated, grad_sq))
    grad_inner_x, grad_state_bc, grad_taps_x, grad_taps_bc = conv_back((grad_sx, grad_sbc))
    pair_low = jnp.stack([grad_gate, grad_inner_x], axis=1).astype(jnp.bfloat16)
    state_low = grad_state_bc.astype(jnp.bfloat16)
    step_low = grad_raw.astype(jnp.bfloat16)
    grad_inner = jnp.einsum("td,tkc->dkc", normed, pair_low, preferred_element_type=jnp.float32)
    grad_state = jnp.einsum("td,ts->ds", normed, state_low, preferred_element_type=jnp.float32)
    grad_step = jnp.einsum("td,th->dh", normed, step_low, preferred_element_type=jnp.float32)
    grad_normed = jnp.einsum(
        "tkc,dkc->td", pair_low, inner_full, preferred_element_type=jnp.float32
    )
    grad_normed = grad_normed + jnp.einsum(
        "ts,ds->td", state_low, state_full, preferred_element_type=jnp.float32
    )
    grad_normed = grad_normed + jnp.einsum(
        "th,dh->td", step_low, step_full, preferred_element_type=jnp.float32
    )
    own_grad = lax.psum_scatter(
        grad_normed.astype(jnp.bfloat16), "head", scatter_dimension=1, tiled=True
    ).astype(jnp.float32)
    own_width = inputs.shape[1]
    start_column = lax.axis_index("head") * own_width
    own_gain = lax.dynamic_slice_in_dim(gain_float, start_column, own_width)
    scaled = own_grad * own_gain[None, :]
    row_part = jnp.sum(scaled * own_inputs, axis=1)
    grad_gain_own = jnp.sum(own_grad * own_inputs * inverse[:, None], axis=0)
    row_total = lax.psum(row_part, "head")
    inverse_cube = inverse * inverse * inverse
    grad_input = (
        cotangent.astype(jnp.float32)
        + inverse[:, None] * scaled
        - own_inputs * (inverse_cube * row_total / D)[:, None]
    )
    grad_gain_full = lax.dynamic_update_slice_in_dim(
        jnp.zeros((D,), jnp.float32), grad_gain_own, start_column, 0
    )
    grad_channel = jnp.concatenate([grad_taps_x, grad_gate_gain[None, :]], axis=0)
    grad_filter = grad_taps_bc.T
    inner_reduced, step_reduced, output_reduced = (
        lax.psum_scatter(grad_inner, "dp", scatter_dimension=0, tiled=True),
        lax.psum_scatter(grad_step, "dp", scatter_dimension=0, tiled=True),
        lax.psum_scatter(block_grad, "dp", scatter_dimension=1, tiled=True),
    )
    state_reduced, gain_reduced, filter_reduced = (
        lax.psum_scatter(grad_state, ("dp", "head"), scatter_dimension=0, tiled=True),
        lax.psum_scatter(grad_gain_full, ("dp", "head"), scatter_dimension=0, tiled=True),
        lax.psum_scatter(grad_filter, ("dp", "head"), scatter_dimension=0, tiled=True),
    )
    channel_reduced, head_reduced = lax.psum((grad_channel, grad_head), "dp")
    total_tokens = inputs.shape[0] * lax.axis_size("dp")
    matrix_rate = RATE_MATRIX / math.sqrt(total_tokens)
    vector_rate = RATE_VECTOR / math.sqrt(total_tokens)
    new_inner = advance(weight_inner, inner_reduced, momentum_inner, average_inner, matrix_rate)
    new_step = advance(weight_step, step_reduced, momentum_step, average_step, matrix_rate)
    new_output = advance(
        weight_output, output_reduced, momentum_output, average_output, matrix_rate
    )
    new_state = advance(weight_state, state_reduced, momentum_state, average_state, matrix_rate)
    new_gain = advance(norm_gain, gain_reduced, momentum_gain, average_gain, vector_rate)
    new_channel = advance(
        channel_table, channel_reduced, momentum_channel, average_channel, vector_rate
    )
    new_head = advance(head_table, head_reduced, momentum_head, average_head, vector_rate)
    new_filter = advance(state_filter, filter_reduced, momentum_filter, average_filter, vector_rate)
    return (
        layer_output,
        grad_input,
        new_inner[0],
        new_inner[1],
        new_inner[2],
        new_step[0],
        new_step[1],
        new_step[2],
        new_output[0],
        new_output[1],
        new_output[2],
        new_state[0],
        new_state[1],
        new_state[2],
        new_gain[0],
        new_gain[1],
        new_gain[2],
        new_channel[0],
        new_channel[1],
        new_channel[2],
        new_head[0],
        new_head[1],
        new_head[2],
        new_filter[0],
        new_filter[1],
        new_filter[2],
    )


def solution(mesh):
    in_specs = (
        P("dp", "head"),
        P("dp", "head"),
        P("dp"),
        P("dp"),
        P("dp"),
        P("dp", None, "head"),
        P("dp", "head"),
        P("head", "dp"),
        P(("dp", "head"), None),
        P(("dp", "head")),
        P(None, "head"),
        P(None, "head"),
        P(("dp", "head"), None),
        P("dp", None, "head"),
        P("dp", "head"),
        P("head", "dp"),
        P(("dp", "head"), None),
        P(("dp", "head")),
        P(None, "head"),
        P(None, "head"),
        P(("dp", "head"), None),
        P("dp", None, "head"),
        P("dp", "head"),
        P("head", "dp"),
        P(("dp", "head"), None),
        P(("dp", "head")),
        P(None, "head"),
        P(None, "head"),
        P(("dp", "head"), None),
    )
    out_specs = (
        P("dp", "head"),
        P("dp", "head"),
        P("dp", None, "head"),
        P("dp", None, "head"),
        P("dp", None, "head"),
        P("dp", "head"),
        P("dp", "head"),
        P("dp", "head"),
        P("head", "dp"),
        P("head", "dp"),
        P("head", "dp"),
        P(("dp", "head"), None),
        P(("dp", "head"), None),
        P(("dp", "head"), None),
        P(("dp", "head")),
        P(("dp", "head")),
        P(("dp", "head")),
        P(None, "head"),
        P(None, "head"),
        P(None, "head"),
        P(None, "head"),
        P(None, "head"),
        P(None, "head"),
        P(("dp", "head"), None),
        P(("dp", "head"), None),
        P(("dp", "head"), None),
    )
    return jax.shard_map(body, mesh=mesh, in_specs=in_specs, out_specs=out_specs, check_vma=False)
```

profile of v0, /device:TPU:0, one launch (start us, length us, event | category | flops | bytes accessed | tf_op | source)
XLA Modules:
  0.0 1316.8 jit_solution(10096558258720219206)
XLA Ops:
  9.6 3.1 copy.409
  16.7 42.3 %all-reduce.20 = bf16[2048]{0:T(1024)(128)(2,1)S(1)} all-reduce(bf16[2048]{0:T(1024)(128)(2,1)S(1)} %dynamic-update-slice), channel_id=1, replica_groups=mesh['dp'=8,'head'=4] {'dp','head'}, use_global_device_ids=true, to_apply=%add.20 | all-reduce | flops 2048 | bytes 8192
  59.1 40.5 %all_gather.24 = bf16[256,5]{1,0:T(8,128)(2,1)S(1)} all-gather(bf16[8,5]{1,0:T(8,128)(2,1)S(1)} %convert_element_type.103), channel_id=1, replica_groups=mesh['dp'=8,'head'=4] {'dp','head'}, dimensions={0}, use_global_device_ids=true | all-gather | bytes 2640 | tf_op jit(solution)/shard_map/all_gather | solution.py:132
  100.0 4.6 mul.844.clone
  104.6 7.7 reshape.331
  112.9 30.9 %all_gather.29 = bf16[2048,16]{0,1:T(8,128)(2,1)S(1)} all-gather(bf16[256,16]{0,1:T(8,128)(2,1)S(1)} %convert_element_type.111), channel_id=1, replica_groups=mesh['dp'=8,'head'=4] {'dp'}, dimensions={0}, use_global_device_ids=true | all-gather | bytes 73728 | tf_op jit(solution)/shard_map/all_gather | solution.py:126
  144.0 3.2 fusion.15
  157.3 4.7 fusion.137
  162.0 70.0 %all-gather.8.cloned.1.call-done = bf16[2048,2,1024]{2,0,1:T(8,128)(2,1)} async-done(((bf16[256,2,1024]{2,0,1:T(8,128)(2,1)}), bf16[2048,2,1024]{2,0,1:T(8,128)(2,1)}) %all-gather.8.cloned.1.call-update) | async-done | bytes 8388624 | tf_op jit(solution)/shard_map/all_gather | solution.py:125
  231.9 12.5 fusion.50
  244.4 3.7 fusion.134
  250.2 3.2 fusion.32
  256.1 8.3 multiply_convert_fusion
  265.5 4.7 reshape.328
  272.7 7.4 reshape.335
  280.1 7.7 copy.278
  287.9 7.7 copy.273
  295.6 3.5 reshape.292
  302.6 4.4 fusion.53
  307.2 23.2 %while.36 = (s32[]{:T(128)}, f32[16,64,128]{2,1,0:T(8,128)S(1)}, f32[4,16,64,128]{3,2,1,0:T(8,128)S(1)}, f32[4]{0:T(128)}, f32[4,16,1,1]{1,3,2,0:T(1,128)}, /*in...) while((s32[]{:T(128)}, f32[16,64,128]{2,1,0:T(8,128)S(1)}, ...), condition=%wide.region_4.5_spmd.clone, body=%wide.region_3.4_spmd.clone.sunk | while | flops 786436 | bytes 2622828 | solution.py:69
  330.4 2.9 fusion.139
  333.4 18.0 %multiply_reduce_fusion.10 = (f32[4,256]{1,0:T(4,128)S(1)}, f32[4,256,16,64]{1,3,2,0:T(8,128)}) fusion(f32[4,256,16,64]{1,3,2,0:T(8,128)S(1)} %copy-done.25, f32[4,256,16]{1,2,0:T(8,128)S(1)} %compare_convert_fusion, f32[4,256,16,64]{1,3,2,0:T(8,128)} %copy.273, f32[16]{0:T(128)S(1)} %copy-done.99, f32[4,256,16,64]{1,3,2,0:T(8,128)S(1)} %fusion.139, ...), kind=kOutput, calls=%fused_computation.102 | convolution fusion | flops 3254778880 | bytes 20254784 | tf_op jit(solution)/shard_map/jvp(ntuh,nuhp->nthp)/dot_general | solution.py:58
  351.4 8.2 copy.333
  359.6 7.6 reshape.334
  367.2 6.6 psum.35
  373.9 14.9 %multiply_reduce_fusion.7 = (f32[1024]{0:T(1024)}, f32[1024]{0:T(1024)S(1)}, f32[1024,1024]{1,0:T(8,128)}, f32[1024,1024]{1,0:T(8,128)}) fusion(f32[1024]{0:T(1024)S(1)} %fusion.121, f32[1024]{0:T(1024)S(1)} %bitcast.298, f32[1024,1024]{1,0:T(8,128)} %reshape.334, f32[1024,2,1024]{2,0,1:T(8,128)} %copy-done.11, ...), kind=kOutput, calls=%fused_computation.98 | convolution fusion | flops 4306499584 | bytes 25182208 | tf_op jit(solution)/shard_map/tw,cw->tc/dot_general | solution.py:189
  388.8 6.0 psum.36
  394.8 12.6 multiply_reduce_fusion.6
  407.4 7.2 reshape.329
  414.6 7.7 copy.281
  422.4 5.7 fusion.54
  429.7 16.3 %while.37 = (s32[]{:T(128)}, f32[16,64,128]{2,1,0:T(8,128)S(1)}, f32[4,16,64,128]{3,2,1,0:T(8,128)}, f32[4,16]{1,0:T(4,128)S(1)}, f32[4,16,64,128]{3,2,1,0:T(8,1...) while((s32[]{:T(128)}, f32[16,64,128]{2,1,0:T(8,128)S(1)}, ...), condition=%wide.region_13.14_spmd.clone, body=%wide.region_11.13_spmd.clone.sunk | while | flops 917492 | bytes 3146284 | solution.py:69
  446.1 3.6 fusion.140
  449.7 7.6 fusion.92
  457.3 22.5 %fusion.14 = (f32[4,256,16]{1,2,0:T(8,128)}, f32[4,256,16]{1,2,0:T(8,128)}, f32[4,256,16]{1,2,0:T(8,128)}, f32[4,256,256]{2,1,0:T(8,128)}) fusion(f32[4,256,16]{1,2,0:T(8,128)S(1)} %bitcast.307, f32[4,256,16]{1,2,0:T(8,128)S(1)} %copy-done.44, f32[4,256,256]{2,1,0:T(8,128)S(1)} %copy-done.37, pred[256,256]{1,0:T(8,128)(4,1)S(1)} %copy-done.68, ...), kind=kOutput, calls=%fused_computation.33 | convolution fusion | flops 3284877312 | bytes 8847360 | tf_op jit(solution)/shard_map/transpose(jvp(ntuh,nuhp->nthp))/dot_general | solution.py:58
  479.7 7.6 fusion.93
  487.3 17.0 %bitcast_add_fusion.3 = f32[4,256,16,64]{1,3,2,0:T(8,128)} fusion(f32[4,256,16,64]{1,3,2,0:T(8,128)S(1)} %fusion.140, f32[4,256,16,64]{1,3,2,0:T(8,128)S(1)} %copy-done.1, f32[4,256,16]{1,2,0:T(8,128)S(1)} %bitcast.308, f32[4,256,16]{1,2,0:T(8,128)S(1)} %copy-done.44, f32[4,256,256]{2,1,0:T(8,128)S(1)} %copy-done.37, pred[256,256]{1,0:T(8,128)(4,1)S(1)} %copy-done.68, ...), kind=kOutput, calls=%fused_computation.79 | convolution fusion | flops 3248488448 | bytes 13959232 | tf_op jit(solution)/shard_map/transpose(jvp(ntuh,nuhp->nthp))/dot_general | solution.py:58
  504.3 3.7 multiply_reduce_fusion.5
  509.5 8.1 copy.328
  517.5 7.6 reshape.330
  531.6 6.2 multiply_reduce_fusion.4
  537.8 5.5 multiply_reduce_fusion.3
  543.4 5.4 slice_multiply_fusion
  555.2 9.9 reduce-window.16
  565.6 3.5 fusion.105
  569.2 9.8 multiply_reduce_fusion.1
  588.1 11.5 fusion.66
  599.6 3.4 fusion.19
  603.1 10.1 convolution_convert_fusion
  613.2 11.5 fusion.128
  624.8 15.4 %fusion.48 = f32[2048,2,1024]{2,0,1:T(8,128)} fusion(bf16[1024,2048]{1,0:T(8,128)(2,1)} %copy-done.5, bf16[1024,1,1024]{2,0,1:T(8,128)(2,1)} %copy-done.33, bf16[1024,1,1024]{2,0,1:T(8,128)(2,1)S(1)} %copy-done.32), kind=kOutput, calls=%fused_computation.92 | convolution fusion | flops 8598323200 | bytes 25165824 | tf_op jit(solution)/shard_map/td,tkc->dkc/dot_general | solution.py:200
  642.2 35.1 %all-reduce.24 = (f32[6,1024]{1,0:T(8,128)S(1)}, f32[3,16]{1,0:T(4,128)S(1)}) all-reduce(f32[6,1024]{1,0:T(8,128)S(1)} %pad_maximum_fusion.4, f32[3,16]{1,0:T(4,128)S(1)} %pad_add_fusion.2), channel_id=1, replica_groups=mesh['dp'=8,'head'=4] {'dp'}, use_global_device_ids=true, to_apply=%region_36.37 | all-reduce | flops 6192 | bytes 49536 | tf_op jit(solution)/shard_map/psum | solution.py:243
  679.9 87.0 %reduce-scatter.18.cloned.1.call-done = f32[64,256]{1,0:T(8,128)} async-done(((f32[2048,256]{1,0:T(8,128)}), f32[64,256]{1,0:T(8,128)}) %reduce-scatter.18.cloned.1.call-update) | async-done | bytes 65552 | tf_op jit(solution)/shard_map/reduce_scatter | solution.py:239
  768.4 41.6 %reduce-scatter.10.cloned.1.call-done = bf16[1024,512]{1,0:T(8,128)(2,1)} async-done(((bf16[1024,2048]{1,0:T(8,128)(2,1)}), bf16[1024,512]{1,0:T(8,128)(2,1)}) %reduce-scatter.10.cloned.1.call-update) | async-done | bytes 1048592 | tf_op jit(solution)/shard_map/reduce_scatter | solution.py:212
  812.5 39.7 %all-reduce.23 = (f32[2048]{0:T(1024)S(1)}, f32[256,5]{0,1:T(8,128)S(1)}) all-reduce(f32[2048]{0:T(1024)S(1)} %dynamic_update_slice.34, f32[256,5]{0,1:T(8,128)S(1)} %add_bitcast_fusion.4), channel_id=8, replica_groups=mesh['dp'=8,'head'=4] {'dp','head'}, use_global_device_ids=true, to_apply=%region_29.30.clone | all-reduce | flops 3328 | bytes 26624
  854.3 6.5 psum.37
  861.6 3.5 fusion.71
  865.1 146.0 %reduce-scatter.16.cloned.1.call-done = f32[1024,256]{1,0:T(8,128)} async-done(((f32[1024,2048]{1,0:T(8,128)}), f32[1024,256]{1,0:T(8,128)}) %reduce-scatter.16.cloned.1.call-update) | async-done | bytes 1048592 | tf_op jit(solution)/shard_map/reduce_scatter | solution.py:236
  1011.1 3.9 multiply_add_fusion.2
  1015.0 280.9 %reduce-scatter.12.cloned.1.call-done = f32[256,2,1024]{2,0,1:T(8,128)} async-done(((f32[2048,2,1024]{2,0,1:T(8,128)}), f32[256,2,1024]{2,0,1:T(8,128)}) %reduce-scatter.12.cloned.1.call-update) | async-done | bytes 2097168 | tf_op jit(solution)/shard_map/reduce_scatter | solution.py:234
  1295.9 5.4 fusion.76
  1301.3 2.9 copy.306
  1304.2 2.9 copy.307
  1307.2 2.9 copy.308
  (408 shorter events, 105.0 us)
Async XLA Ops:
  7.2 7.5 copy-start.26
  7.2 136.8 %all-gather.6.cloned.1.call-start = ((), (), s32[]{:S(2)}) async-start(), calls=%async_computation.6 | async-start | bytes 5242880 | tf_op jit(solution)/shard_map/all_gather | solution.py:136
  8.0 149.3 %all-gather.10.cloned.1.call-start = ((), (), s32[]{:S(2)}) async-start(), calls=%async_computation.8 | async-start | bytes 1081344 | tf_op jit(solution)/shard_map/all_gather | solution.py:130
  9.5 6.8 copy-start.104
  9.5 6.8 copy-start.45
  9.5 6.8 copy-start.100
  9.5 49.4 %copy-start.105 = (s32[4]{0:T(128)S(1)}, s32[4]{0:T(128)}, u32[]{:S(2)}) copy-start(s32[4]{0:T(128)} %param.36) | copy-start | bytes 52
  9.6 49.5 %copy-start.86 = (f32[8,5]{1,0:T(8,128)S(1)}, f32[8,5]{1,0:T(8,128)}, u32[]{:S(2)}) copy-start(f32[8,5]{1,0:T(8,128)} %param.45) | copy-start | bytes 484
  9.6 222.4 %all-gather.8.cloned.1.call-start = ((), (), s32[]{:S(2)}) async-start(), calls=%async_computation.7 | async-start | bytes 9437184 | tf_op jit(solution)/shard_map/all_gather | solution.py:125
  12.8 361.1 %all-gather.14.cloned.1.call-start = ((), (), s32[]{:S(2)}) async-start(), calls=%async_computation.11 | async-start | bytes 5242880 | tf_op jit(solution)/shard_map/all_gather | solution.py:188
  14.6 359.2 %all-gather.12.cloned.1.call-start = ((), (), s32[]{:S(2)}) async-start(), calls=%async_computation.9 | async-start | bytes 4718592 | tf_op jit(solution)/shard_map/all_gather | solution.py:127
  15.6 663.0 %reduce-scatter.14.cloned.1.call-start = ((), (), s32[]{:S(2)}) async-start(), calls=%async_computation.14 | async-start | bytes 147456 | tf_op jit(solution)/shard_map/reduce_scatter | solution.py:235
  59.0 40.7 %copy-start.78 = (bf16[2048]{0:T(1024)(128)(2,1)}, bf16[2048]{0:T(1024)(128)(2,1)S(1)}, u32[]{:S(2)}) copy-start(bf16[2048]{0:T(1024)(128)(2,1)S(1)} %all-reduce.20) | copy-start | bytes 12292
  59.0 40.7 %copy-start.80 = (f32[4]{0:T(128)}, f32[4]{0:T(128)S(1)}, u32[]{:S(2)}) copy-start(f32[4]{0:T(128)S(1)} %convert_element_type.110) | copy-start | bytes 52
  59.1 194.3 %copy-start.72 = (f32[1024]{0:T(1024)}, f32[1024]{0:T(1024)S(1)}, u32[]{:S(2)}) copy-start(f32[1024]{0:T(1024)S(1)} %get-tuple-element.532) | copy-start | bytes 12292
  59.1 194.3 %copy-start.74 = (f32[1024]{0:T(1024)}, f32[1024]{0:T(1024)S(1)}, u32[]{:S(2)}) copy-start(f32[1024]{0:T(1024)S(1)} %get-tuple-element.534) | copy-start | bytes 12292
  104.6 7.7 copy-start.90
  104.6 8.2 copy-start.66
  112.8 35.7 %copy-start.88 = (f32[16]{0:T(128)}, f32[16]{0:T(128)S(1)}, u32[]{:S(2)}) copy-start(f32[16]{0:T(128)S(1)} %get-tuple-element.536) | copy-start | bytes 196
  143.9 109.5 %copy-start.51 = (f32[1280]{0:T(1024)}, f32[1280]{0:T(1024)S(1)}, u32[]{:S(2)}) copy-start(f32[1280]{0:T(1024)S(1)} %get-tuple-element.434) | copy-start | bytes 15364
  143.9 109.5 %copy-start.53 = (f32[1280]{0:T(1024)}, f32[1280]{0:T(1024)S(1)}, u32[]{:S(2)}) copy-start(f32[1280]{0:T(1024)S(1)} %get-tuple-element.431) | copy-start | bytes 15364
  143.9 109.5 %copy-start.55 = (f32[1280]{0:T(1024)}, f32[1280]{0:T(1024)S(1)}, u32[]{:S(2)}) copy-start(f32[1280]{0:T(1024)S(1)} %get-tuple-element.432) | copy-start | bytes 15364
  144.0 109.5 %copy-start.57 = (f32[1280]{0:T(1024)}, f32[1280]{0:T(1024)S(1)}, u32[]{:S(2)}) copy-start(f32[1280]{0:T(1024)S(1)} %get-tuple-element.433) | copy-start | bytes 15364
  162.0 91.5 %copy-start.8 = (f32[1024,256]{1,0:T(8,128)}, f32[1024,256]{1,0:T(8,128)S(1)}, u32[]{:S(2)}) copy-start(f32[1024,256]{1,0:T(8,128)S(1)} %fusion.137) | copy-start | bytes 3145732
  333.4 18.1 %copy-start.16 = (f32[4,256,16,64]{1,3,2,0:T(8,128)}, f32[4,256,16,64]{1,3,2,0:T(8,128)S(1)}, u32[]{:S(2)}) copy-start(f32[4,256,16,64]{1,3,2,0:T(8,128)S(1)} %fusion.139) | copy-start | bytes 12582916
  414.6 7.7 copy-start.24
  422.4 7.3 copy-start.106
  449.7 7.6 copy-start.1
  449.7 7.6 copy-start.37
  525.1 12.6 slice-start
  525.1 12.7 slice-start.2
  551.7 13.7 %copy-start.40 = (f32[1024,16]{0,1:T(8,128)S(1)}, f32[1024,16]{0,1:T(8,128)}, u32[]{:S(2)}) copy-start(f32[1024,16]{0,1:T(8,128)} %get-tuple-element.538) | copy-start | bytes 196612
  551.7 13.7 %copy-start.89 = (f32[16]{0:T(128)S(1)}, f32[16]{0:T(128)}, u32[]{:S(2)}) copy-start(f32[16]{0:T(128)} %copy-done.88) | copy-start | bytes 196
  554.6 14.6 %copy-start.9 = (f32[1024,256]{1,0:T(8,128)S(1)}, f32[1024,256]{1,0:T(8,128)}, u32[]{:S(2)}) copy-start(f32[1024,256]{1,0:T(8,128)} %copy-done.8) | copy-start | bytes 3145732
  554.6 14.6 %copy-start.58 = (f32[1280]{0:T(1024)S(1)}, f32[1280]{0:T(1024)}, u32[]{:S(2)}) copy-start(f32[1280]{0:T(1024)} %copy-done.57) | copy-start | bytes 15364
  569.2 197.7 %reduce-scatter.18.cloned.1.call-start = ((), (), s32[]{:S(2)}) async-start(), calls=%async_computation.16 | async-start | bytes 2162688 | tf_op jit(solution)/shard_map/reduce_scatter | solution.py:239
  569.2 11.3 copy-start.6
  583.2 226.8 %reduce-scatter.10.cloned.1.call-start = ((), (), s32[]{:S(2)}) async-start(), calls=%async_computation.12 | async-start | bytes 5242880 | tf_op jit(solution)/shard_map/reduce_scatter | solution.py:212
  588.1 11.5 copy-start.39
  603.0 258.5 %reduce-scatter.8.cloned.1.call-start = ((), (), s32[]{:S(2)}) async-start(), calls=%async_computation.10 | async-start | bytes 5242880 | tf_op jit(solution)/shard_map/reduce_scatter | solution.py:182
  613.2 398.0 %reduce-scatter.16.cloned.1.call-start = ((), (), s32[]{:S(2)}) async-start(), calls=%async_computation.15 | async-start | bytes 9437184 | tf_op jit(solution)/shard_map/reduce_scatter | solution.py:236
  624.7 671.2 %reduce-scatter.12.cloned.1.call-start = ((), (), s32[]{:S(2)}) async-start(), calls=%async_computation.13 | async-start | bytes 18874368 | tf_op jit(solution)/shard_map/reduce_scatter | solution.py:234
  640.2 37.1 %copy-start.91 = (f32[3,16]{1,0:T(4,128)S(1)}, f32[3,16]{1,0:T(4,128)}, u32[]{:S(2)}) copy-start(f32[3,16]{1,0:T(4,128)} %param.44) | copy-start | bytes 580
  640.2 37.1 %copy-start.97 = (f32[3,16]{1,0:T(4,128)S(1)}, f32[3,16]{1,0:T(4,128)}, u32[]{:S(2)}) copy-start(f32[3,16]{1,0:T(4,128)} %param.60) | copy-start | bytes 580
  640.2 37.1 %copy-start.98 = (f32[3,16]{1,0:T(4,128)S(1)}, f32[3,16]{1,0:T(4,128)}, u32[]{:S(2)}) copy-start(f32[3,16]{1,0:T(4,128)} %param.52) | copy-start | bytes 580
  640.2 37.6 %copy-start.46 = (f32[6,1024]{1,0:T(8,128)S(1)}, f32[6,1024]{1,0:T(8,128)}, u32[]{:S(2)}) copy-start(f32[6,1024]{1,0:T(8,128)} %param.43) | copy-start | bytes 73732
  640.2 37.6 %copy-start.76 = (f32[6,1024]{1,0:T(8,128)S(1)}, f32[6,1024]{1,0:T(8,128)}, u32[]{:S(2)}) copy-start(f32[6,1024]{1,0:T(8,128)} %param.59) | copy-start | bytes 73732
  640.2 37.6 %copy-start.77 = (f32[6,1024]{1,0:T(8,128)S(1)}, f32[6,1024]{1,0:T(8,128)}, u32[]{:S(2)}) copy-start(f32[6,1024]{1,0:T(8,128)} %param.51) | copy-start | bytes 73732
  640.3 38.3 %copy-start.67 = (f32[256,16]{0,1:T(8,128)S(1)}, f32[256,16]{0,1:T(8,128)}, u32[]{:S(2)}) copy-start(f32[256,16]{0,1:T(8,128)} %param.39) | copy-start | bytes 49156
  640.3 38.3 %copy-start.84 = (f32[256,16]{0,1:T(8,128)S(1)}, f32[256,16]{0,1:T(8,128)}, u32[]{:S(2)}) copy-start(f32[256,16]{0,1:T(8,128)} %param.55) | copy-start | bytes 49156
  640.3 38.3 %copy-start.85 = (f32[256,16]{0,1:T(8,128)S(1)}, f32[256,16]{0,1:T(8,128)}, u32[]{:S(2)}) copy-start(f32[256,16]{0,1:T(8,128)} %param.47) | copy-start | bytes 49156
  640.3 126.6 %copy-start.42 = (f32[64,256]{1,0:T(8,128)S(1)}, f32[64,256]{1,0:T(8,128)}, u32[]{:S(2)}) copy-start(f32[64,256]{1,0:T(8,128)} %param.41) | copy-start | bytes 196612
  640.3 126.6 %copy-start.61 = (f32[64,256]{1,0:T(8,128)S(1)}, f32[64,256]{1,0:T(8,128)}, u32[]{:S(2)}) copy-start(f32[64,256]{1,0:T(8,128)} %param.57) | copy-start | bytes 196612
  640.3 126.6 %copy-start.62 = (f32[64,256]{1,0:T(8,128)S(1)}, f32[64,256]{1,0:T(8,128)}, u32[]{:S(2)}) copy-start(f32[64,256]{1,0:T(8,128)} %param.49) | copy-start | bytes 196612
  640.3 169.7 %copy-start.20 = (bf16[1024,512]{1,0:T(8,128)(2,1)S(1)}, bf16[1024,512]{1,0:T(8,128)(2,1)}, u32[]{:S(2)}) copy-start(bf16[1024,512]{1,0:T(8,128)(2,1)} %param.33) | copy-start | bytes 3145732
  640.3 169.7 %copy-start.60 = (f32[1024]{0:T(1024)S(1)}, f32[1024]{0:T(1024)}, u32[]{:S(2)}) copy-start(f32[1024]{0:T(1024)} %copy-done.59) | copy-start | bytes 12292
  640.3 220.5 %copy-start.101 = (f32[64]{0:T(128)S(1)}, f32[64]{0:T(128)}, u32[]{:S(2)}) copy-start(f32[64]{0:T(128)} %param.42) | copy-start | bytes 772
  640.4 220.5 %copy-start.102 = (f32[64]{0:T(128)S(1)}, f32[64]{0:T(128)}, u32[]{:S(2)}) copy-start(f32[64]{0:T(128)} %param.58) | copy-start | bytes 772
  640.4 220.5 %copy-start.103 = (f32[64]{0:T(128)S(1)}, f32[64]{0:T(128)}, u32[]{:S(2)}) copy-start(f32[64]{0:T(128)} %param.50) | copy-start | bytes 772
  640.4 221.1 %copy-start.71 = (f32[1024]{0:T(1024)S(1)}, f32[1024]{0:T(1024)}, u32[]{:S(2)}) copy-start(f32[1024]{0:T(1024)} %copy-done.70) | copy-start | bytes 12292
  640.4 221.1 %copy-start.83 = (f32[1024]{0:T(1024)S(1)}, f32[1024]{0:T(1024)}, u32[]{:S(2)}) copy-start(f32[1024]{0:T(1024)} %get-tuple-element.530) | copy-start | bytes 12292
  640.4 221.1 %copy-start.29 = (bf16[1024,512]{1,0:T(8,128)(2,1)S(1)}, bf16[1024,512]{1,0:T(8,128)(2,1)}, u32[]{:S(2)}) copy-start(bf16[1024,512]{1,0:T(8,128)(2,1)} %param.34) | copy-start | bytes 3145732
  812.2 198.9 %copy-start.27 = (f32[1024,256]{1,0:T(8,128)S(1)}, f32[1024,256]{1,0:T(8,128)}, u32[]{:S(2)}) copy-start(f32[1024,256]{1,0:T(8,128)} %param.40) | copy-start | bytes 3145732
  865.1 430.8 %copy-start.21 = (f32[256,2,1024]{2,1,0:T(2,128)S(1)}, f32[256,2,1024]{2,1,0:T(2,128)}, u32[]{:S(2)}) copy-start(f32[256,2,1024]{2,1,0:T(2,128)} %param.38) | copy-start | bytes 6291460
  (58 other events, 198.7 us)
Sparse Core Ops, SparseCore 0:
  9.6 37.8 all-gather.5
  51.0 53.7 all-gather.9
  107.6 124.3 all-gather.7
  233.9 32.6 all-gather.13
  269.1 75.0 all-gather.11
  569.3 58.8 reduce-scatter.13
  631.0 135.8 reduce-scatter.17
  769.6 40.4 reduce-scatter.9
  812.6 45.1 reduce-scatter.7
  861.7 149.3 reduce-scatter.15
  1014.9 280.9 reduce-scatter.11
where the time goes:
time: 1330 us; the launch traced here: 1320 us
  waiting for transfers between devices  626 us (47%)
  blocking collectives  208 us (16%)
  matrix products  191 us (14%)
  local copies, waits for them, and re-layouts  141 us (11%)
  other arithmetic  134 us (10%)
  between operations  15.7 us (1%)
    reduce_scatter x1, waiting for transfers between devices, body(): lax.psum_scatter(grad_inner, 'dp', scatter_dimension=0, tiled=True)  281 us
    reduce_scatter x1, waiting for transfers between devices, body(): lax.psum_scatter(block_grad, 'dp', scatter_dimension=1, tiled=True)  146 us
    reduce_scatter x1, waiting for transfers between devices, body(): lax.psum_scatter(grad_state, ('dp', 'head'), scatter_dimension=0, tiled=T...  87 us
    unnamed x2, blocking collectives  82 us
    all_gather x1, waiting for transfers between devices, body(): lax.all_gather(weight_inner.astype(jnp.bfloat16), 'dp', axis=0, tiled=True)  70 us
    dot_general x3, matrix products, state_mixer(): jnp.einsum('ntuh,nuhp->nthp', mixing, values, precision=HIGHEST)  57.4 us
    reduce_scatter x1, waiting for transfers between devices, body(): lax.psum_scatter(grad_normed.astype(jnp.bfloat16), 'head', scatter_dimens...  41.6 us
    all_gather x1, blocking collectives, body(): lax.all_gather(state_filter.astype(jnp.bfloat16), ('dp', 'head'), axis=0,...  40.5 us
  transfers between devices with their start and end apart: 11, of which 5 were waited for; matrix products, arithmetic and copies ran while one was open for 19% of the time, Pallas kernels for 0%

commit v1 on v0

--- a/solution.py
+++ b/solution.py
@@ -17,6 +17,18 @@
 RATE_MATRIX = 0.02
 RATE_VECTOR = 0.1
 HIGHEST = lax.Precision.HIGHEST
+
+
+def collect(value, axis, dim):
+    ways, here, hop = (lax.axis_size(axis), lax.axis_index(axis), value.shape[dim])
+    line, have = (value, 1)
+    while have < ways:
+        line = jnp.concatenate(
+            [line, lax.ppermute(line, axis, [(d, (d - have) % ways) for d in range(ways)])],
+            axis=dim,
+        )
+        have = 2 * have
+    return jnp.roll(line, here * hop, axis=dim)
 
 
 def rounded(value):
@@ -123,7 +135,7 @@
 ):
     inner_full, step_full, output_full = (
         lax.all_gather(weight_inner.astype(jnp.bfloat16), "dp", axis=0, tiled=True),
-        lax.all_gather(weight_step.astype(jnp.bfloat16), "dp", axis=0, tiled=True),
+        collect(weight_step.astype(jnp.bfloat16), "dp", 0),
         lax.all_gather(weight_output.astype(jnp.bfloat16), "dp", axis=1, tiled=True),
     )
     state_full, gain_full, filter_full = (

time: 1330 us -> 1330 us (level)
  blocking collectives: 208 us -> 170 us
  waiting for transfers between devices: 626 us -> 657 us
    all_gather x1 -> x0, blocking collectives: 30.9 us -> none  [body(): lax.all_gather(weight_step.astype(jnp.bfloat16), 'dp', axis=0, tiled=True)]
    all_gather x1, waiting for transfers between devices: 70 us -> 93.1 us  [body(): lax.all_gather(weight_inner.astype(jnp.bfloat16), 'dp', axis=0, tiled=True)]
  transfers between devices with their start and end apart: 11 -> 14, of which waited for: 5 -> 7; matrix products, arithmetic and copies ran while one was open for 19% -> 19% of each run, Pallas kernels for 0% -> 0%
where the time goes in v1:
time: 1330 us; the launch traced here: 1320 us
  waiting for transfers between devices  657 us (49%)
  matrix products  190 us (14%)
  blocking collectives  170 us (13%)
  local copies, waits for them, and re-layouts  141 us (11%)
  other arithmetic  135 us (10%)
  between operations  15.8 us (1%)
    reduce_scatter x1, waiting for transfers between devices, body(): lax.psum_scatter(grad_inner, 'dp', scatter_dimension=0, tiled=True)  281 us
    reduce_scatter x1, waiting for transfers between devices, body(): lax.psum_scatter(block_grad, 'dp', scatter_dimension=1, tiled=True)  146 us
    all_gather x1, waiting for transfers between devices, body(): lax.all_gather(weight_inner.astype(jnp.bfloat16), 'dp', axis=0, tiled=True)  93.1 us
    reduce_scatter x1, waiting for transfers between devices, body(): lax.psum_scatter(grad_state, ('dp', 'head'), scatter_dimension=0, tiled=T...  87.2 us
    unnamed x2, blocking collectives  76.8 us
    dot_general x3, matrix products, state_mixer(): jnp.einsum('ntuh,nuhp->nthp', mixing, values, precision=HIGHEST)  57.4 us
    reduce_scatter x1, waiting for transfers between devices, body(): lax.psum_scatter(grad_normed.astype(jnp.bfloat16), 'head', scatter_dimens...  41.7 us
    all_gather x1, blocking collectives, body(): lax.all_gather(state_filter.astype(jnp.bfloat16), ('dp', 'head'), axis=0,...  38.5 us
  transfers between devices with their start and end apart: 14, of which 7 were waited for; matrix products, arithmetic and copies ran while one was open for 19% of the time, Pallas kernels for 0%

profile of v1, /device:TPU:0, one launch (start us, length us, event | category | flops | bytes accessed | tf_op | source)
XLA Modules:
  0.0 1318.6 jit_solution(14255489760456519159)
XLA Ops:
  9.6 3.1 copy.409
  14.7 6.1 collective-permute-start
  22.6 38.5 %all_gather.21 = bf16[256,5]{1,0:T(8,128)(2,1)S(1)} all-gather(bf16[8,5]{1,0:T(8,128)(2,1)S(1)} %convert_element_type.103), channel_id=1, replica_groups=mesh['dp'=8,'head'=4] {'dp','head'}, dimensions={0}, use_global_device_ids=true | all-gather | bytes 2640 | tf_op jit(solution)/shard_map/all_gather | solution.py:144
  62.1 37.1 %all-reduce.20 = bf16[2048]{0:T(1024)(128)(2,1)S(1)} all-reduce(bf16[2048]{0:T(1024)(128)(2,1)S(1)} %dynamic-update-slice), channel_id=1, replica_groups=mesh['dp'=8,'head'=4] {'dp','head'}, use_global_device_ids=true, to_apply=%add.20 | all-reduce | flops 2048 | bytes 8192
  99.4 4.6 mul.848.clone
  104.0 7.7 reshape.331
  118.5 4.3 collective-permute-done.2
  122.9 3.3 fusion.15
  136.3 3.7 fusion.141
  140.0 93.1 %all-gather.8.cloned.1.call-done = bf16[2048,2,1024]{2,0,1:T(8,128)(2,1)} async-done(((bf16[256,2,1024]{2,0,1:T(8,128)(2,1)}), bf16[2048,2,1024]{2,0,1:T(8,128)(2,1)}) %all-gather.8.cloned.1.call-update) | async-done | bytes 8388624 | tf_op jit(solution)/shard_map/all_gather | solution.py:137
  233.1 12.5 fusion.50
  245.6 3.8 fusion.138
  251.3 3.2 fusion.32
  257.2 8.3 multiply_convert_fusion
  266.7 4.7 reshape.328
  273.9 7.4 reshape.335
  281.3 7.7 copy.278
  289.0 7.7 copy.273
  296.7 3.5 reshape.292
  303.7 4.4 fusion.53
  308.3 23.3 %while.36 = (s32[]{:T(128)}, f32[16,64,128]{2,1,0:T(8,128)S(1)}, f32[4,16,64,128]{3,2,1,0:T(8,128)S(1)}, f32[4]{0:T(128)}, f32[4,16,1,1]{1,3,2,0:T(1,128)}, /*in...) while((s32[]{:T(128)}, f32[16,64,128]{2,1,0:T(8,128)S(1)}, ...), condition=%wide.region_4.5_spmd.clone, body=%wide.region_3.4_spmd.clone.sunk | while | flops 786436 | bytes 2622828 | solution.py:81
  331.7 2.9 fusion.143
  334.7 18.0 %multiply_reduce_fusion.10 = (f32[4,256]{1,0:T(4,128)S(1)}, f32[4,256,16,64]{1,3,2,0:T(8,128)}) fusion(f32[4,256,16,64]{1,3,2,0:T(8,128)S(1)} %copy-done.25, f32[4,256,16]{1,2,0:T(8,128)S(1)} %compare_convert_fusion, f32[4,256,16,64]{1,3,2,0:T(8,128)} %copy.273, f32[16]{0:T(128)S(1)} %copy-done.99, f32[4,256,16,64]{1,3,2,0:T(8,128)S(1)} %fusion.143, ...), kind=kOutput, calls=%fused_computation.102 | convolution fusion | flops 3254778880 | bytes 20254784 | tf_op jit(solution)/shard_map/jvp(ntuh,nuhp->nthp)/dot_general | solution.py:70
  352.7 8.1 copy.333
  360.8 7.6 reshape.334
  368.4 6.6 psum.35
  375.1 14.9 %multiply_reduce_fusion.7 = (f32[1024]{0:T(1024)}, f32[1024]{0:T(1024)S(1)}, f32[1024,1024]{1,0:T(8,128)}, f32[1024,1024]{1,0:T(8,128)}) fusion(f32[1024]{0:T(1024)S(1)} %fusion.123, f32[1024]{0:T(1024)S(1)} %bitcast.296, f32[1024,1024]{1,0:T(8,128)} %reshape.334, f32[1024,2,1024]{2,0,1:T(8,128)} %copy-done.11, ...), kind=kOutput, calls=%fused_computation.98 | convolution fusion | flops 4306499584 | bytes 25182208 | tf_op jit(solution)/shard_map/tw,cw->tc/dot_general | solution.py:201
  390.0 6.0 psum.36
  396.0 12.6 multiply_reduce_fusion.6
  408.6 7.2 reshape.329
  415.9 7.7 copy.281
  423.6 5.7 fusion.54
  430.9 16.3 %while.37 = (s32[]{:T(128)}, f32[16,64,128]{2,1,0:T(8,128)S(1)}, f32[4,16,64,128]{3,2,1,0:T(8,128)}, f32[4,16]{1,0:T(4,128)S(1)}, f32[4,16,64,128]{3,2,1,0:T(8,1...) while((s32[]{:T(128)}, f32[16,64,128]{2,1,0:T(8,128)S(1)}, ...), condition=%wide.region_13.14_spmd.clone, body=%wide.region_11.13_spmd.clone.sunk | while | flops 917492 | bytes 3146284 | solution.py:81
  447.3 3.6 fusion.144
  450.9 7.6 fusion.92
  458.5 22.5 %fusion.14 = (f32[4,256,16]{1,2,0:T(8,128)}, f32[4,256,16]{1,2,0:T(8,128)}, f32[4,256,16]{1,2,0:T(8,128)}, f32[4,256,256]{2,1,0:T(8,128)}) fusion(f32[4,256,16]{1,2,0:T(8,128)S(1)} %bitcast.305, f32[4,256,16]{1,2,0:T(8,128)S(1)} %copy-done.44, f32[4,256,256]{2,1,0:T(8,128)S(1)} %copy-done.37, pred[256,256]{1,0:T(8,128)(4,1)S(1)} %copy-done.68, ...), kind=kOutput, calls=%fused_computation.33 | convolution fusion | flops 3284877312 | bytes 8847360 | tf_op jit(solution)/shard_map/transpose(jvp(ntuh,nuhp->nthp))/dot_general | solution.py:70
  481.0 7.6 fusion.93
  488.6 17.0 %bitcast_add_fusion.3 = f32[4,256,16,64]{1,3,2,0:T(8,128)} fusion(f32[4,256,16,64]{1,3,2,0:T(8,128)S(1)} %fusion.144, f32[4,256,16,64]{1,3,2,0:T(8,128)S(1)} %copy-done.1, f32[4,256,16]{1,2,0:T(8,128)S(1)} %bitcast.306, f32[4,256,16]{1,2,0:T(8,128)S(1)} %copy-done.44, f32[4,256,256]{2,1,0:T(8,128)S(1)} %copy-done.37, pred[256,256]{1,0:T(8,128)(4,1)S(1)} %copy-done.68, ...), kind=kOutput, calls=%fused_computation.79 | convolution fusion | flops 3248488448 | bytes 13959232 | tf_op jit(solution)/shard_map/transpose(jvp(ntuh,nuhp->nthp))/dot_general | solution.py:70
  505.5 3.7 multiply_reduce_fusion.5
  510.7 8.0 copy.328
  518.7 7.6 reshape.330
  532.8 6.2 multiply_reduce_fusion.4
  539.1 5.6 multiply_reduce_fusion.3
  544.7 5.4 slice_multiply_fusion
  556.5 9.9 reduce-window.16
  566.9 3.5 fusion.107
  570.5 9.8 multiply_reduce_fusion.1
  589.3 11.5 fusion.66
  600.9 3.4 fusion.19
  604.3 10.1 convolution_convert_fusion
  614.5 11.5 fusion.132
  626.1 15.4 %fusion.48 = f32[2048,2,1024]{2,0,1:T(8,128)} fusion(bf16[1024,2048]{1,0:T(8,128)(2,1)} %copy-done.5, bf16[1024,1,1024]{2,0,1:T(8,128)(2,1)} %copy-done.33, bf16[1024,1,1024]{2,0,1:T(8,128)(2,1)S(1)} %copy-done.32), kind=kOutput, calls=%fused_computation.92 | convolution fusion | flops 8598323200 | bytes 25165824 | tf_op jit(solution)/shard_map/td,tkc->dkc/dot_general | solution.py:212
  643.5 35.1 %all-reduce.24 = (f32[6,1024]{1,0:T(8,128)S(1)}, f32[3,16]{1,0:T(4,128)S(1)}) all-reduce(f32[6,1024]{1,0:T(8,128)S(1)} %pad_maximum_fusion.5, f32[3,16]{1,0:T(4,128)S(1)} %pad_add_fusion.2), channel_id=1, replica_groups=mesh['dp'=8,'head'=4] {'dp'}, use_global_device_ids=true, to_apply=%region_36.37 | all-reduce | flops 6192 | bytes 49536 | tf_op jit(solution)/shard_map/psum | solution.py:255
  681.2 87.2 %reduce-scatter.18.cloned.1.call-done = f32[64,256]{1,0:T(8,128)} async-done(((f32[2048,256]{1,0:T(8,128)}), f32[64,256]{1,0:T(8,128)}) %reduce-scatter.18.cloned.1.call-update) | async-done | bytes 65552 | tf_op jit(solution)/shard_map/reduce_scatter | solution.py:251
  770.0 41.7 %reduce-scatter.10.cloned.1.call-done = bf16[1024,512]{1,0:T(8,128)(2,1)} async-done(((bf16[1024,2048]{1,0:T(8,128)(2,1)}), bf16[1024,512]{1,0:T(8,128)(2,1)}) %reduce-scatter.10.cloned.1.call-update) | async-done | bytes 1048592 | tf_op jit(solution)/shard_map/reduce_scatter | solution.py:224
  814.1 39.7 %all-reduce.23 = (f32[2048]{0:T(1024)S(1)}, f32[256,5]{0,1:T(8,128)S(1)}) all-reduce(f32[2048]{0:T(1024)S(1)} %dynamic_update_slice.34, f32[256,5]{0,1:T(8,128)S(1)} %add_bitcast_fusion.4), channel_id=8, replica_groups=mesh['dp'=8,'head'=4] {'dp','head'}, use_global_device_ids=true, to_apply=%region_29.30.clone | all-reduce | flops 3328 | bytes 26624
  855.9 6.6 psum.37
  863.2 3.5 fusion.71
  866.7 146.1 %reduce-scatter.16.cloned.1.call-done = f32[1024,256]{1,0:T(8,128)} async-done(((f32[1024,2048]{1,0:T(8,128)}), f32[1024,256]{1,0:T(8,128)}) %reduce-scatter.16.cloned.1.call-update) | async-done | bytes 1048592 | tf_op jit(solution)/shard_map/reduce_scatter | solution.py:248
  1012.8 3.8 multiply_add_fusion.2
  1016.6 281.1 %reduce-scatter.12.cloned.1.call-done = f32[256,2,1024]{2,0,1:T(8,128)} async-done(((f32[2048,2,1024]{2,0,1:T(8,128)}), f32[256,2,1024]{2,0,1:T(8,128)}) %reduce-scatter.12.cloned.1.call-update) | async-done | bytes 2097168 | tf_op jit(solution)/shard_map/reduce_scatter | solution.py:246
  1297.7 5.4 fusion.76
  1303.1 2.9 copy.306
  1309.0 2.9 copy.308
  (422 shorter events, 114.7 us)
Async XLA Ops:
  7.2 13.5 %copy-start.26 = (f32[1024,256]{1,0:T(8,128)S(1)}, f32[1024,256]{1,0:T(8,128)}, u32[]{:S(2)}) copy-start(f32[1024,256]{1,0:T(8,128)} %param.40) | copy-start | bytes 3145732
  7.2 115.7 %all-gather.6.cloned.1.call-start = ((), (), s32[]{:S(2)}) async-start(), calls=%async_computation.6 | async-start | bytes 5242880 | tf_op jit(solution)/shard_map/all_gather | solution.py:148
  8.0 128.3 %all-gather.10.cloned.1.call-start = ((), (), s32[]{:S(2)}) async-start(), calls=%async_computation.8 | async-start | bytes 1081344 | tf_op jit(solution)/shard_map/all_gather | solution.py:142
  9.5 12.9 copy-start.104
  9.5 12.9 copy-start.105
  9.5 13.0 copy-start.86
  9.6 51.5 %copy-start.88 = (f32[3,16]{1,0:T(4,128)S(1)}, f32[3,16]{1,0:T(4,128)}, u32[]{:S(2)}) copy-start(f32[3,16]{1,0:T(4,128)} %param.44) | copy-start | bytes 580
  9.6 223.5 %all-gather.8.cloned.1.call-start = ((), (), s32[]{:S(2)}) async-start(), calls=%async_computation.7 | async-start | bytes 9437184 | tf_op jit(solution)/shard_map/all_gather | solution.py:137
  12.8 49.0 %copy-start.45 = (f32[6,1024]{1,0:T(8,128)S(1)}, f32[6,1024]{1,0:T(8,128)}, u32[]{:S(2)}) copy-start(f32[6,1024]{1,0:T(8,128)} %param.43) | copy-start | bytes 73732
  12.8 49.0 %copy-start.100 = (f32[64]{0:T(128)S(1)}, f32[64]{0:T(128)}, u32[]{:S(2)}) copy-start(f32[64]{0:T(128)} %param.42) | copy-start | bytes 772
  12.8 362.3 %all-gather.14.cloned.1.call-start = ((), (), s32[]{:S(2)}) async-start(), calls=%async_computation.11 | async-start | bytes 5242880 | tf_op jit(solution)/shard_map/all_gather | solution.py:200
  14.6 360.5 %all-gather.12.cloned.1.call-start = ((), (), s32[]{:S(2)}) async-start(), calls=%async_computation.9 | async-start | bytes 4718592 | tf_op jit(solution)/shard_map/all_gather | solution.py:139
  14.7 97.1 %collective-permute-start = (bf16[256,16]{0,1:T(8,128)(2,1)S(1)}, bf16[256,16]{0,1:T(8,128)(2,1)S(1)}, u32[]{:S(2)}, u32[]{:S(2)}) collective-permute-start(bf16[256,16]{0,1:T(8,128)(2,1)S(1)} %get-tuple-element.507), channel_id=1, source_target_pairs={{0,28},{4,0},{8,4},{12,8},{16,12},{20,16},{24,20},{28,24},{1,29},{... | collective-permute-start | bytes 24584 | tf_op jit(solution)/shard_map/ppermute | solution.py:27
  21.6 658.2 %reduce-scatter.14.cloned.1.call-start = ((), (), s32[]{:S(2)}) async-start(), calls=%async_computation.14 | async-start | bytes 147456 | tf_op jit(solution)/shard_map/reduce_scatter | solution.py:247
  22.4 39.7 %copy-start.80 = (f32[4]{0:T(128)}, f32[4]{0:T(128)S(1)}, u32[]{:S(2)}) copy-start(f32[4]{0:T(128)S(1)} %convert_element_type.110) | copy-start | bytes 52
  22.5 232.0 %copy-start.72 = (f32[1024]{0:T(1024)}, f32[1024]{0:T(1024)S(1)}, u32[]{:S(2)}) copy-start(f32[1024]{0:T(1024)S(1)} %get-tuple-element.534) | copy-start | bytes 12292
  22.5 232.0 %copy-start.74 = (f32[1024]{0:T(1024)}, f32[1024]{0:T(1024)S(1)}, u32[]{:S(2)}) copy-start(f32[1024]{0:T(1024)S(1)} %get-tuple-element.536) | copy-start | bytes 12292
  61.6 65.9 %copy-start.90 = (f32[16]{0:T(128)}, f32[16]{0:T(128)S(1)}, u32[]{:S(2)}) copy-start(f32[16]{0:T(128)S(1)} %get-tuple-element.538) | copy-start | bytes 196
  111.8 142.8 %copy-start.51 = (f32[1280]{0:T(1024)}, f32[1280]{0:T(1024)S(1)}, u32[]{:S(2)}) copy-start(f32[1280]{0:T(1024)S(1)} %get-tuple-element.434) | copy-start | bytes 15364
  111.8 142.8 %copy-start.53 = (f32[1280]{0:T(1024)}, f32[1280]{0:T(1024)S(1)}, u32[]{:S(2)}) copy-start(f32[1280]{0:T(1024)S(1)} %get-tuple-element.431) | copy-start | bytes 15364
  111.8 142.8 %copy-start.55 = (f32[1280]{0:T(1024)}, f32[1280]{0:T(1024)S(1)}, u32[]{:S(2)}) copy-start(f32[1280]{0:T(1024)S(1)} %get-tuple-element.432) | copy-start | bytes 15364
  111.8 142.8 %copy-start.57 = (f32[1280]{0:T(1024)}, f32[1280]{0:T(1024)S(1)}, u32[]{:S(2)}) copy-start(f32[1280]{0:T(1024)S(1)} %get-tuple-element.433) | copy-start | bytes 15364
  111.8 4.6 collective-permute-start.1
  116.5 6.4 collective-permute-start.2
  140.0 114.6 %copy-start.8 = (f32[1024,256]{1,0:T(8,128)}, f32[1024,256]{1,0:T(8,128)S(1)}, u32[]{:S(2)}) copy-start(f32[1024,256]{1,0:T(8,128)S(1)} %fusion.141) | copy-start | bytes 3145732
  334.6 18.0 %copy-start.17 = (f32[4,256,16,64]{1,3,2,0:T(8,128)}, f32[4,256,16,64]{1,3,2,0:T(8,128)S(1)}, u32[]{:S(2)}) copy-start(f32[4,256,16,64]{1,3,2,0:T(8,128)S(1)} %fusion.143) | copy-start | bytes 12582916
  415.9 7.7 copy-start.24
  450.9 7.6 copy-start.1
  450.9 7.6 copy-start.37
  526.3 12.6 slice-start
  526.3 12.7 slice-start.2
  553.0 13.7 %copy-start.38 = (f32[1024,16]{0,1:T(8,128)S(1)}, f32[1024,16]{0,1:T(8,128)}, u32[]{:S(2)}) copy-start(f32[1024,16]{0,1:T(8,128)} %get-tuple-element.540) | copy-start | bytes 196612
  553.0 13.7 %copy-start.91 = (f32[16]{0:T(128)S(1)}, f32[16]{0:T(128)}, u32[]{:S(2)}) copy-start(f32[16]{0:T(128)} %copy-done.90) | copy-start | bytes 196
  555.9 14.6 %copy-start.9 = (f32[1024,256]{1,0:T(8,128)S(1)}, f32[1024,256]{1,0:T(8,128)}, u32[]{:S(2)}) copy-start(f32[1024,256]{1,0:T(8,128)} %copy-done.8) | copy-start | bytes 3145732
  555.9 14.6 %copy-start.58 = (f32[1280]{0:T(1024)S(1)}, f32[1280]{0:T(1024)}, u32[]{:S(2)}) copy-start(f32[1280]{0:T(1024)} %copy-done.57) | copy-start | bytes 15364
  570.4 198.0 %reduce-scatter.18.cloned.1.call-start = ((), (), s32[]{:S(2)}) async-start(), calls=%async_computation.16 | async-start | bytes 2162688 | tf_op jit(solution)/shard_map/reduce_scatter | solution.py:251
  570.5 11.3 copy-start.6
  584.5 227.2 %reduce-scatter.10.cloned.1.call-start = ((), (), s32[]{:S(2)}) async-start(), calls=%async_computation.12 | async-start | bytes 5242880 | tf_op jit(solution)/shard_map/reduce_scatter | solution.py:224
  589.3 11.5 copy-start.42
  604.3 258.9 %reduce-scatter.8.cloned.1.call-start = ((), (), s32[]{:S(2)}) async-start(), calls=%async_computation.10 | async-start | bytes 5242880 | tf_op jit(solution)/shard_map/reduce_scatter | solution.py:194
  614.5 398.3 %reduce-scatter.16.cloned.1.call-start = ((), (), s32[]{:S(2)}) async-start(), calls=%async_computation.15 | async-start | bytes 9437184 | tf_op jit(solution)/shard_map/reduce_scatter | solution.py:248
  626.0 671.7 %reduce-scatter.12.cloned.1.call-start = ((), (), s32[]{:S(2)}) async-start(), calls=%async_computation.13 | async-start | bytes 18874368 | tf_op jit(solution)/shard_map/reduce_scatter | solution.py:246
  641.5 37.1 %copy-start.89 = (f32[3,16]{1,0:T(4,128)S(1)}, f32[3,16]{1,0:T(4,128)}, u32[]{:S(2)}) copy-start(f32[3,16]{1,0:T(4,128)} %param.44) | copy-start | bytes 580
  641.5 37.1 %copy-start.97 = (f32[3,16]{1,0:T(4,128)S(1)}, f32[3,16]{1,0:T(4,128)}, u32[]{:S(2)}) copy-start(f32[3,16]{1,0:T(4,128)} %param.60) | copy-start | bytes 580
  641.5 37.1 %copy-start.98 = (f32[3,16]{1,0:T(4,128)S(1)}, f32[3,16]{1,0:T(4,128)}, u32[]{:S(2)}) copy-start(f32[3,16]{1,0:T(4,128)} %param.52) | copy-start | bytes 580
  641.5 37.7 %copy-start.46 = (f32[6,1024]{1,0:T(8,128)S(1)}, f32[6,1024]{1,0:T(8,128)}, u32[]{:S(2)}) copy-start(f32[6,1024]{1,0:T(8,128)} %param.43) | copy-start | bytes 73732
  641.5 37.7 %copy-start.76 = (f32[6,1024]{1,0:T(8,128)S(1)}, f32[6,1024]{1,0:T(8,128)}, u32[]{:S(2)}) copy-start(f32[6,1024]{1,0:T(8,128)} %param.59) | copy-start | bytes 73732
  641.5 37.7 %copy-start.77 = (f32[6,1024]{1,0:T(8,128)S(1)}, f32[6,1024]{1,0:T(8,128)}, u32[]{:S(2)}) copy-start(f32[6,1024]{1,0:T(8,128)} %param.51) | copy-start | bytes 73732
  641.5 38.3 %copy-start.67 = (f32[256,16]{0,1:T(8,128)S(1)}, f32[256,16]{0,1:T(8,128)}, u32[]{:S(2)}) copy-start(f32[256,16]{0,1:T(8,128)} %param.39) | copy-start | bytes 49156
  641.6 38.3 %copy-start.84 = (f32[256,16]{0,1:T(8,128)S(1)}, f32[256,16]{0,1:T(8,128)}, u32[]{:S(2)}) copy-start(f32[256,16]{0,1:T(8,128)} %param.55) | copy-start | bytes 49156
  641.6 38.3 %copy-start.85 = (f32[256,16]{0,1:T(8,128)S(1)}, f32[256,16]{0,1:T(8,128)}, u32[]{:S(2)}) copy-start(f32[256,16]{0,1:T(8,128)} %param.47) | copy-start | bytes 49156
  641.6 126.8 %copy-start.40 = (f32[64,256]{1,0:T(8,128)S(1)}, f32[64,256]{1,0:T(8,128)}, u32[]{:S(2)}) copy-start(f32[64,256]{1,0:T(8,128)} %param.41) | copy-start | bytes 196612
  641.6 126.8 %copy-start.61 = (f32[64,256]{1,0:T(8,128)S(1)}, f32[64,256]{1,0:T(8,128)}, u32[]{:S(2)}) copy-start(f32[64,256]{1,0:T(8,128)} %param.57) | copy-start | bytes 196612
  641.6 126.8 %copy-start.62 = (f32[64,256]{1,0:T(8,128)S(1)}, f32[64,256]{1,0:T(8,128)}, u32[]{:S(2)}) copy-start(f32[64,256]{1,0:T(8,128)} %param.49) | copy-start | bytes 196612
  641.6 170.0 %copy-start.20 = (bf16[1024,512]{1,0:T(8,128)(2,1)S(1)}, bf16[1024,512]{1,0:T(8,128)(2,1)}, u32[]{:S(2)}) copy-start(bf16[1024,512]{1,0:T(8,128)(2,1)} %param.33) | copy-start | bytes 3145732
  641.6 170.0 %copy-start.60 = (f32[1024]{0:T(1024)S(1)}, f32[1024]{0:T(1024)}, u32[]{:S(2)}) copy-start(f32[1024]{0:T(1024)} %copy-done.59) | copy-start | bytes 12292
  641.6 220.9 %copy-start.101 = (f32[64]{0:T(128)S(1)}, f32[64]{0:T(128)}, u32[]{:S(2)}) copy-start(f32[64]{0:T(128)} %param.42) | copy-start | bytes 772
  641.7 220.9 %copy-start.102 = (f32[64]{0:T(128)S(1)}, f32[64]{0:T(128)}, u32[]{:S(2)}) copy-start(f32[64]{0:T(128)} %param.58) | copy-start | bytes 772
  641.7 220.8 %copy-start.103 = (f32[64]{0:T(128)S(1)}, f32[64]{0:T(128)}, u32[]{:S(2)}) copy-start(f32[64]{0:T(128)} %param.50) | copy-start | bytes 772
  641.7 221.4 %copy-start.71 = (f32[1024]{0:T(1024)S(1)}, f32[1024]{0:T(1024)}, u32[]{:S(2)}) copy-start(f32[1024]{0:T(1024)} %copy-done.70) | copy-start | bytes 12292
  641.7 221.5 %copy-start.83 = (f32[1024]{0:T(1024)S(1)}, f32[1024]{0:T(1024)}, u32[]{:S(2)}) copy-start(f32[1024]{0:T(1024)} %get-tuple-element.532) | copy-start | bytes 12292
  641.7 221.5 %copy-start.29 = (bf16[1024,512]{1,0:T(8,128)(2,1)S(1)}, bf16[1024,512]{1,0:T(8,128)(2,1)}, u32[]{:S(2)}) copy-start(bf16[1024,512]{1,0:T(8,128)(2,1)} %param.34) | copy-start | bytes 3145732
  813.8 199.0 %copy-start.27 = (f32[1024,256]{1,0:T(8,128)S(1)}, f32[1024,256]{1,0:T(8,128)}, u32[]{:S(2)}) copy-start(f32[1024,256]{1,0:T(8,128)} %param.40) | copy-start | bytes 3145732
  866.7 431.0 %copy-start.21 = (f32[256,2,1024]{2,1,0:T(2,128)S(1)}, f32[256,2,1024]{2,1,0:T(2,128)}, u32[]{:S(2)}) copy-start(f32[256,2,1024]{2,1,0:T(2,128)} %param.38) | copy-start | bytes 6291460
  (61 other events, 218.7 us)
Sparse Core Ops, SparseCore 0:
  9.6 37.6 all-gather.5
  50.8 53.9 all-gather.9
  107.5 125.5 all-gather.7
  235.1 32.6 all-gather.13
  270.3 75.0 all-gather.11
  570.5 59.1 reduce-scatter.13
  632.6 135.7 reduce-scatter.17
  771.1 40.5 reduce-scatter.9
  814.2 45.1 reduce-scatter.7
  863.3 149.4 reduce-scatter.15
  1016.6 281.0 reduce-scatter.11
